TPU v7x, 256 devices: a whole 4x4x8 slice. The times are simulated.
256 devices in a mesh: sens: 4 (over z_lo, core), par: 64 (over z_hi, x, y).
Axes of the slice: x: 4, y: 4, z: 8 (z_hi: 4, z_lo: 2; z = z_hi * 2 + z_lo), core: 2. Of those that a mesh axis runs over, the one named last changes fastest.
Arguments:
- model: bfloat16 [4, 1024, 256], P('sens', 'par'), may hold values from -6 to 6
- kernel: bfloat16 [512, 1024, 256], P('sens', 'par'), may hold values from -0.01171875 to 0.01171875
- observed: float32 [4, 512, 256], P(None, 'sens'), may hold values from -6 to 6
- weights: float32 [512], P('sens'), may hold values from 0.25 to 4
Outputs:
- gradient: float32 [4, 1024, 256], P('sens', 'par')
- misfit: float32 [], replicated
All inputs are finite; a program needn't handle non-finite values.
Results may differ from a plain program's by a relative error of at most 0.0027.
Values may be sent and summed in bfloat16 or wider, within the bound.
A program may use at most 192 MiB of HBM per device.

v0:
```python
import jax
import jax.numpy as jnp
from jax import lax
from jax.sharding import PartitionSpec as P


def causal_rows(series):
    length_steps = series.shape[-1]
    padded = jnp.concatenate([series, jnp.zeros_like(series)], axis=-1)
    reps = (1,) * (series.ndim - 1) + (length_steps,)
    flat = jnp.tile(padded, reps)
    stride = 2 * length_steps - 1
    flat = flat[..., : length_steps * stride].reshape(series.shape[:-1] + (length_steps, stride))
    return flat[..., :length_steps]


def leading_rows(series):
    length_steps = series.shape[-1]
    padded = jnp.concatenate([series, jnp.zeros_like(series)], axis=-1)
    reps = (1,) * (series.ndim - 1) + (length_steps + 1,)
    flat = jnp.tile(padded, reps)
    stride = 2 * length_steps + 1
    flat = flat[..., : length_steps * stride].reshape(series.shape[:-1] + (length_steps, stride))
    return flat[..., :length_steps]


def local(model, kernel, observed, weights):
    full_model = lax.all_gather(model, "sens", axis=0, tiled=True)
    toeplitz_operator = causal_rows(full_model)
    summed_terms = jnp.einsum(
        "oua,luaz->loz", kernel, toeplitz_operator, preferred_element_type=jnp.float32
    )
    vectors = full_model.shape[0]
    sensors = weights.shape[0]
    steps = full_model.shape[2]
    entries = vectors * sensors * lax.axis_size("sens") * steps
    predicted = lax.psum(summed_terms, "par")
    mismatch = predicted - observed
    weighted_residual = weights[None, :, None] * mismatch
    residual = weighted_residual.astype(jnp.bfloat16)
    squared = lax.psum(jnp.sum(weighted_residual * mismatch), "sens")
    misfit = 0.5 * squared / entries

    def single_adjoint(series):
        shifted = leading_rows(series)
        return jnp.einsum("spk,skt->pt", kernel, shifted, preferred_element_type=jnp.float32)

    adjoint_pieces = lax.map(single_adjoint, residual)
    gradient = lax.psum_scatter(adjoint_pieces, "sens", scatter_dimension=0, tiled=True)
    return (gradient, misfit)


def solution(mesh):
    return jax.shard_map(
        local,
        mesh=mesh,
        in_specs=(P("sens", "par", None), P("sens", "par", None), P(None, "sens", None), P("sens")),
        out_specs=(P("sens", "par", None), P()),
        check_vma=False,
    )
```

profile of v0, /device:TPU:1, one launch (start us, length us, event | category | flops | bytes accessed | tf_op | source)
XLA Modules:
  0.0 1190.9 jit_solution(9768342964295590249)
XLA Ops:
  7.2 0.0 all-reduce.4.cloned.1.call-start
  7.2 8.4 all_gather.3
  15.7 5.9 tile.8
  21.6 17.0 %tile.9 = bf16[4,16,131072]{2,1,0:T(8,128)(2,1)} reshape(bf16[4,16,256,512]{3,2,1,0:T(8,128)(2,1)} %tile.8) | data formatting | bytes 33554432 | tf_op jit(solution)/shard_map/tile | solution.py:11
  38.6 13.7 %slice.16 = bf16[4,16,130816]{2,1,0:T(8,128)(2,1)} slice(bf16[4,16,131072]{2,1,0:T(8,128)(2,1)} %tile.9), slice={[0:4], [0:16], [0:130816]} | slice | bytes 33488896 | tf_op jit(solution)/shard_map/slice | solution.py:13
  52.3 36.2 %reshape.19 = bf16[4,16,256,511]{3,2,1,0:T(8,128)(2,1)} reshape(bf16[4,16,130816]{2,1,0:T(8,128)(2,1)} %slice.16) | data formatting | bytes 33488896 | tf_op jit(solution)/shard_map/reshape | solution.py:13
  88.5 6.6 fusion.10
  95.1 0.0 all-reduce.4.cloned.1.call-update
  95.1 0.0 reduce-scatter.2.cloned.1.call-start
  95.2 1.6 copy.19
  96.8 0.2 copy.18
  97.0 688.3 %all-reduce.4.cloned.1.call-done = f32[4,128,256]{1,2,0:T(8,128)} async-done(((f32[4,128,256]{1,2,0:T(8,128)}), f32[4,128,256]{1,2,0:T(8,128)}) %all-reduce.4.cloned.1.call-update) | async-done | bytes 524304 | tf_op jit(solution)/shard_map/psum | solution.py:37
  785.3 1.9 fusion.15
  787.2 332.0 %while.10 = (s32[]{:T(128)}, f32[4,16,256]{2,1,0:T(8,128)}, bf16[4,128,256]{1,2,0:T(8,128)(2,1)S(1)}, bf16[128,16,256]{0,1,2:T(8,128)(2,1)S(1)}, s32[]{:T(128)}, /*index=5*/bf16[]{:T(256)}) while((s32[]{:T(128)}, f32[4,16,256]{2,1,0:T(8,128)}, bf16[4,128,256]{1,2,0:T(8,128)(2,1)S(1)}, bf16[128,16,256]{0,1,2:T(8,128)(2,1)S(1)}, s32[]{:T(128)}, ...), condition=%wide.region_2.0_spmd, body=%wide.region_1.0_spmd.sunk | while | flops 268435456 | bytes 186466896 | solution.py:48
  787.2 13.5 %tile.21 = bf16[128,257,512]{0,2,1:T(8,128)(2,1)} broadcast(bf16[128,512]{0,1:T(8,128)(2,1)S(1)} %concatenate.8), dimensions={0,2} | broadcast | bytes 33816576 | tf_op jit(solution)/shard_map/while/body/eval_jaxpr/tile | solution.py:21
  800.8 22.9 %slice.31 = bf16[128,131328]{0,1:T(8,128)(2,1)} slice(bf16[128,131584]{0,1:T(8,128)(2,1)} %bitcast.32), slice={[0:128], [0:131328]} | slice | bytes 67239936 | tf_op jit(solution)/shard_map/while/body/eval_jaxpr/slice | solution.py:23
  823.6 37.7 %reshape.24 = bf16[128,256,513]{0,2,1:T(8,128)(2,1)} reshape(bf16[128,131328]{0,1:T(8,128)(2,1)} %slice.31) | data formatting | bytes 67239936 | tf_op jit(solution)/shard_map/while/body/eval_jaxpr/reshape | solution.py:23
  861.3 8.9 fusion.22
  870.2 13.5 %tile.21 = bf16[128,257,512]{0,2,1:T(8,128)(2,1)} broadcast(bf16[128,512]{0,1:T(8,128)(2,1)S(1)} %concatenate.8), dimensions={0,2} | broadcast | bytes 33816576 | tf_op jit(solution)/shard_map/while/body/eval_jaxpr/tile | solution.py:21
  883.7 22.9 %slice.31 = bf16[128,131328]{0,1:T(8,128)(2,1)} slice(bf16[128,131584]{0,1:T(8,128)(2,1)} %bitcast.32), slice={[0:128], [0:131328]} | slice | bytes 67239936 | tf_op jit(solution)/shard_map/while/body/eval_jaxpr/slice | solution.py:23
  906.6 37.7 %reshape.24 = bf16[128,256,513]{0,2,1:T(8,128)(2,1)} reshape(bf16[128,131328]{0,1:T(8,128)(2,1)} %slice.31) | data formatting | bytes 67239936 | tf_op jit(solution)/shard_map/while/body/eval_jaxpr/reshape | solution.py:23
  944.3 8.9 fusion.22
  953.2 13.5 %tile.21 = bf16[128,257,512]{0,2,1:T(8,128)(2,1)} broadcast(bf16[128,512]{0,1:T(8,128)(2,1)S(1)} %concatenate.8), dimensions={0,2} | broadcast | bytes 33816576 | tf_op jit(solution)/shard_map/while/body/eval_jaxpr/tile | solution.py:21
  966.7 22.9 %slice.31 = bf16[128,131328]{0,1:T(8,128)(2,1)} slice(bf16[128,131584]{0,1:T(8,128)(2,1)} %bitcast.32), slice={[0:128], [0:131328]} | slice | bytes 67239936 | tf_op jit(solution)/shard_map/while/body/eval_jaxpr/slice | solution.py:23
  989.6 37.7 %reshape.24 = bf16[128,256,513]{0,2,1:T(8,128)(2,1)} reshape(bf16[128,131328]{0,1:T(8,128)(2,1)} %slice.31) | data formatting | bytes 67239936 | tf_op jit(solution)/shard_map/while/body/eval_jaxpr/reshape | solution.py:23
  1027.2 8.9 fusion.22
  1036.2 13.5 %tile.21 = bf16[128,257,512]{0,2,1:T(8,128)(2,1)} broadcast(bf16[128,512]{0,1:T(8,128)(2,1)S(1)} %concatenate.8), dimensions={0,2} | broadcast | bytes 33816576 | tf_op jit(solution)/shard_map/while/body/eval_jaxpr/tile | solution.py:21
  1049.7 22.9 %slice.31 = bf16[128,131328]{0,1:T(8,128)(2,1)} slice(bf16[128,131584]{0,1:T(8,128)(2,1)} %bitcast.32), slice={[0:128], [0:131328]} | slice | bytes 67239936 | tf_op jit(solution)/shard_map/while/body/eval_jaxpr/slice | solution.py:23
  1072.6 37.7 %reshape.24 = bf16[128,256,513]{0,2,1:T(8,128)(2,1)} reshape(bf16[128,131328]{0,1:T(8,128)(2,1)} %slice.31) | data formatting | bytes 67239936 | tf_op jit(solution)/shard_map/while/body/eval_jaxpr/reshape | solution.py:23
  1110.2 8.9 fusion.22
  1119.2 51.3 %psum.15 = f32[]{:T(128)} all-reduce(f32[]{:T(128)} %get-tuple-element.45), channel_id=1, replica_groups=mesh['sens'=4,'par'=64] {'sens'}, use_global_device_ids=true, to_apply=%region_5.6 | all-reduce | flops 1 | bytes 8 | tf_op jit(solution)/shard_map/psum | solution.py:41
  1171.1 11.8 reduce-scatter.2.cloned.1.call-done
  (17 shorter events, 0.1 us)
Async XLA Ops:
  7.2 778.2 %all-reduce.4.cloned.1.call-start = ((), (), s32[]{:S(2)}) async-start(), calls=%async_computation.1 | async-start | bytes 1048576 | tf_op jit(solution)/shard_map/psum | solution.py:37
  52.3 36.2 %copy-start = (bf16[128,16,256]{2,1,0:T(8,128)(2,1)S(1)}, bf16[128,16,256]{2,1,0:T(8,128)(2,1)}, u32[]{:S(2)}) copy-start(bf16[128,16,256]{2,1,0:T(8,128)(2,1)} %param.7) | copy-start | bytes 3145732
  88.5 8.4 copy-start.1
  88.5 696.9 %copy-start.2 = (f32[128]{0:T(128)S(1)}, f32[128]{0:T(128)}, u32[]{:S(2)}) copy-start(f32[128]{0:T(128)} %param.9) | copy-start | bytes 1540
  95.1 1087.8 %reduce-scatter.2.cloned.1.call-start = ((), (), s32[]{:S(2)}) async-start(), calls=%async_computation.2 | async-start | bytes 81920 | tf_op jit(solution)/shard_map/reduce_scatter | solution.py:49
Sparse Core Ops, SparseCore 0:
  95.2 690.0 all-reduce.3
  1119.3 63.6 reduce-scatter.1
where the time goes:
time: 1200 us; the launch traced here: 1190 us
  waiting for transfers between devices  700 us (58%)
  local copies, waits for them, and re-layouts  371 us (31%)
  blocking collectives  59.7 us (5%)
  matrix products  42.3 us (4%)
  between operations  15.9 us (1%)
    psum x1, waiting for transfers between devices, local(): predicted = lax.psum(summed_terms, 'par')  688 us
    reshape x4, local copies, waits for them, and re-layouts, leading_rows(): flat[..., :length_steps * stride]  151 us
    slice x4, local copies, waits for them, and re-layouts, leading_rows(): flat[..., :length_steps * stride]  91.4 us
    another operation x4, local copies, waits for them, and re-layouts, leading_rows(): flat = jnp.tile(padded, reps)  54.2 us
    psum x1, blocking collectives, local(): squared = lax.psum(jnp.sum(weighted_residual * mismatch), 'sens')  51.3 us
    reshape x1, local copies, waits for them, and re-layouts, causal_rows(): flat[..., :length_steps * stride]  36.2 us
    dot_general x4, matrix products, single_adjoint(): jnp.einsum('spk,skt->pt', kernel, shifted, preferred_element_type=jnp.flo...  35.6 us
  transfers between devices with their start and end apart: 2, of which 2 were waited for; matrix products, arithmetic and copies ran while one was open for 0% of the time, Pallas kernels for 0%

commit v1 on v0

--- a/solution.py
+++ b/solution.py
@@ -2,6 +2,11 @@
 import jax.numpy as jnp
 from jax import lax
 from jax.sharding import PartitionSpec as P
+
+
+def wall_see(content):
+    u1 = jax.lax.all_gather(content, "par").sum(axis=0)
+    return u1
 
 
 def causal_rows(series):
@@ -34,7 +39,7 @@
     sensors = weights.shape[0]
     steps = full_model.shape[2]
     entries = vectors * sensors * lax.axis_size("sens") * steps
-    predicted = lax.psum(summed_terms, "par")
+    predicted = wall_see(summed_terms)
     mismatch = predicted - observed
     weighted_residual = weights[None, :, None] * mismatch
     residual = weighted_residual.astype(jnp.bfloat16)

time: 1200 us -> 759 us (0.63)
  waiting for transfers between devices: 700 us -> 297 us
  blocking collectives: 59.7 us -> 16 us
    psum x1 -> x0, waiting for transfers between devices: 688 us -> none  [local(): predicted = lax.psum(summed_terms, 'par')]
    all_gather x0 -> x1, waiting for transfers between devices: none -> 285 us  [wall_see(): u1 = jax.lax.all_gather(content, 'par').sum(axis=0)]
    psum x1, blocking collectives: 51.3 us -> 7.59 us  [local(): squared = lax.psum(jnp.sum(weighted_residual * mismatch), 'sens')]
where the time goes in v1:
time: 759 us; the launch traced here: 755 us
  local copies, waits for them, and re-layouts  372 us (49%)
  waiting for transfers between devices  297 us (39%)
  matrix products  41.4 us (5%)
  blocking collectives  16 us (2%)
  between operations  15.9 us (2%)
  other arithmetic  12.8 us (2%)
    all_gather x1, waiting for transfers between devices, wall_see(): u1 = jax.lax.all_gather(content, 'par').sum(axis=0)  285 us
    reshape x4, local copies, waits for them, and re-layouts, leading_rows(): flat[..., :length_steps * stride]  151 us
    slice x4, local copies, waits for them, and re-layouts, leading_rows(): flat[..., :length_steps * stride]  91.4 us
    another operation x4, local copies, waits for them, and re-layouts, leading_rows(): flat = jnp.tile(padded, reps)  54.2 us
    reshape x1, local copies, waits for them, and re-layouts, causal_rows(): flat[..., :length_steps * stride]  36.2 us
    dot_general x4, matrix products, single_adjoint(): jnp.einsum('spk,skt->pt', kernel, shifted, preferred_element_type=jnp.flo...  35.6 us
    another operation x2, local copies, waits for them, and re-layouts, causal_rows(): flat = jnp.tile(padded, reps)  22.9 us
  transfers between devices with their start and end apart: 2, of which 2 were waited for; matrix products, arithmetic and copies ran while one was open for 0% of the time, Pallas kernels for 0%

profile of v1, /device:TPU:1, one launch (start us, length us, event | category | flops | bytes accessed | tf_op | source)
XLA Modules:
  0.0 755.1 jit_solution(12834045957249988192)
XLA Ops:
  7.2 8.4 %all_gather.9 = bf16[4,16,256]{2,1,0:T(8,128)(2,1)S(1)} all-gather(bf16[1,16,256]{2,1,0:T(8,128)(2,1)} %param.6), channel_id=1, replica_groups=mesh['sens'=4,'par'=64] {'sens'}, dimensions={0}, use_global_device_ids=true | all-gather | bytes 40960 | tf_op jit(solution)/shard_map/all_gather | solution.py:33
  15.7 5.9 tile.8
  21.6 17.0 %tile.9 = bf16[4,16,131072]{2,1,0:T(8,128)(2,1)} reshape(bf16[4,16,256,512]{3,2,1,0:T(8,128)(2,1)} %tile.8) | data formatting | bytes 33554432 | tf_op jit(solution)/shard_map/tile | solution.py:16
  38.6 13.7 %slice.16 = bf16[4,16,130816]{2,1,0:T(8,128)(2,1)} slice(bf16[4,16,131072]{2,1,0:T(8,128)(2,1)} %tile.9), slice={[0:4], [0:16], [0:130816]} | slice | bytes 33488896 | tf_op jit(solution)/shard_map/slice | solution.py:18
  52.3 36.2 %reshape.19 = bf16[4,16,256,511]{3,2,1,0:T(8,128)(2,1)} reshape(bf16[4,16,130816]{2,1,0:T(8,128)(2,1)} %slice.16) | data formatting | bytes 33488896 | tf_op jit(solution)/shard_map/reshape | solution.py:18
  88.5 5.8 fusion.10
  94.2 1.0 copy.22
  95.3 1.6 copy.24
  97.0 284.8 %all-gather.3.cloned.1.call-done = f32[256,128,256]{2,1,0:T(8,128)} async-done(((f32[4,128,256]{2,1,0:T(8,128)}), f32[256,128,256]{2,1,0:T(8,128)}) %all-gather.3.cloned.1.call-update) | async-done | bytes 33554448 | tf_op jit(solution)/shard_map/all_gather | solution.py:8
  381.8 11.9 %reduce_sum.18 = f32[4,128,256]{2,1,0:T(8,128)S(1)} reduce(f32[64,4,128,256]{3,2,1,0:T(8,128)} %bitcast.33, f32[]{:T(128)} %constant.5.clone.1), dimensions={0}, to_apply=%region_0.0 | reduce | flops 8257536 | bytes 34078724 | tf_op jit(solution)/shard_map/reduce_sum | solution.py:8
  393.7 0.9 fusion.15
  394.6 332.5 %while.10 = (s32[]{:T(128)}, f32[4,16,256]{2,1,0:T(8,128)}, bf16[4,128,256]{2,1,0:T(8,128)(2,1)S(1)}, bf16[128,16,256]{0,1,2:T(8,128)(2,1)S(1)}, s32[]{:T(128)}, /*index=5*/bf16[]{:T(256)}) while((s32[]{:T(128)}, f32[4,16,256]{2,1,0:T(8,128)}, bf16[4,128,256]{2,1,0:T(8,128)(2,1)S(1)}, bf16[128,16,256]{0,1,2:T(8,128)(2,1)S(1)}, s32[]{:T(128)}, ...), condition=%wide.region_2.0_spmd, body=%wide.region_1.0_spmd.sunk | while | flops 268435456 | bytes 186597968 | solution.py:53
  394.8 13.5 %tile.21 = bf16[128,257,512]{0,2,1:T(8,128)(2,1)} broadcast(bf16[128,512]{0,1:T(8,128)(2,1)S(1)} %concatenate.8), dimensions={0,2} | broadcast | bytes 33816576 | tf_op jit(solution)/shard_map/while/body/eval_jaxpr/tile | solution.py:26
  408.3 22.9 %slice.31 = bf16[128,131328]{0,1:T(8,128)(2,1)} slice(bf16[128,131584]{0,1:T(8,128)(2,1)} %bitcast.32), slice={[0:128], [0:131328]} | slice | bytes 67239936 | tf_op jit(solution)/shard_map/while/body/eval_jaxpr/slice | solution.py:28
  431.2 37.7 %reshape.25 = bf16[128,256,513]{0,2,1:T(8,128)(2,1)} reshape(bf16[128,131328]{0,1:T(8,128)(2,1)} %slice.31) | data formatting | bytes 67239936 | tf_op jit(solution)/shard_map/while/body/eval_jaxpr/reshape | solution.py:28
  468.8 8.9 %fusion.22 = f32[4,16,256]{2,1,0:T(8,128)} fusion(f32[4,16,256]{2,1,0:T(8,128)} %get-tuple-element.83, s32[]{:T(128)} %get-tuple-element.82, bf16[128,16,256]{0,1,2:T(8,128)(2,1)S(1)} %get-tuple-element.91, bf16[128,256,513]{0,2,1:T(8,128)(2,1)} %reshape.25), kind=kOutput, calls=%fused_computation.3.clone.1 | convolution fusion | flops 268435456 | bytes 17842688 | tf_op jit(solution)/shard_map/while/body/eval_jaxpr/spk,skt->pt/dot_general | solution.py:51
  477.7 0.1 copy.34
  477.9 13.5 %tile.21 = bf16[128,257,512]{0,2,1:T(8,128)(2,1)} broadcast(bf16[128,512]{0,1:T(8,128)(2,1)S(1)} %concatenate.8), dimensions={0,2} | broadcast | bytes 33816576 | tf_op jit(solution)/shard_map/while/body/eval_jaxpr/tile | solution.py:26
  491.4 22.9 %slice.31 = bf16[128,131328]{0,1:T(8,128)(2,1)} slice(bf16[128,131584]{0,1:T(8,128)(2,1)} %bitcast.32), slice={[0:128], [0:131328]} | slice | bytes 67239936 | tf_op jit(solution)/shard_map/while/body/eval_jaxpr/slice | solution.py:28
  514.3 37.7 %reshape.25 = bf16[128,256,513]{0,2,1:T(8,128)(2,1)} reshape(bf16[128,131328]{0,1:T(8,128)(2,1)} %slice.31) | data formatting | bytes 67239936 | tf_op jit(solution)/shard_map/while/body/eval_jaxpr/reshape | solution.py:28
  551.9 8.9 %fusion.22 = f32[4,16,256]{2,1,0:T(8,128)} fusion(f32[4,16,256]{2,1,0:T(8,128)} %get-tuple-element.83, s32[]{:T(128)} %get-tuple-element.82, bf16[128,16,256]{0,1,2:T(8,128)(2,1)S(1)} %get-tuple-element.91, bf16[128,256,513]{0,2,1:T(8,128)(2,1)} %reshape.25), kind=kOutput, calls=%fused_computation.3.clone.1 | convolution fusion | flops 268435456 | bytes 17842688 | tf_op jit(solution)/shard_map/while/body/eval_jaxpr/spk,skt->pt/dot_general | solution.py:51
  560.9 0.1 copy.34
  561.0 13.5 %tile.21 = bf16[128,257,512]{0,2,1:T(8,128)(2,1)} broadcast(bf16[128,512]{0,1:T(8,128)(2,1)S(1)} %concatenate.8), dimensions={0,2} | broadcast | bytes 33816576 | tf_op jit(solution)/shard_map/while/body/eval_jaxpr/tile | solution.py:26
  574.5 22.9 %slice.31 = bf16[128,131328]{0,1:T(8,128)(2,1)} slice(bf16[128,131584]{0,1:T(8,128)(2,1)} %bitcast.32), slice={[0:128], [0:131328]} | slice | bytes 67239936 | tf_op jit(solution)/shard_map/while/body/eval_jaxpr/slice | solution.py:28
  597.4 37.7 %reshape.25 = bf16[128,256,513]{0,2,1:T(8,128)(2,1)} reshape(bf16[128,131328]{0,1:T(8,128)(2,1)} %slice.31) | data formatting | bytes 67239936 | tf_op jit(solution)/shard_map/while/body/eval_jaxpr/reshape | solution.py:28
  635.1 8.9 %fusion.22 = f32[4,16,256]{2,1,0:T(8,128)} fusion(f32[4,16,256]{2,1,0:T(8,128)} %get-tuple-element.83, s32[]{:T(128)} %get-tuple-element.82, bf16[128,16,256]{0,1,2:T(8,128)(2,1)S(1)} %get-tuple-element.91, bf16[128,256,513]{0,2,1:T(8,128)(2,1)} %reshape.25), kind=kOutput, calls=%fused_computation.3.clone.1 | convolution fusion | flops 268435456 | bytes 17842688 | tf_op jit(solution)/shard_map/while/body/eval_jaxpr/spk,skt->pt/dot_general | solution.py:51
  644.1 13.5 %tile.21 = bf16[128,257,512]{0,2,1:T(8,128)(2,1)} broadcast(bf16[128,512]{0,1:T(8,128)(2,1)S(1)} %concatenate.8), dimensions={0,2} | broadcast | bytes 33816576 | tf_op jit(solution)/shard_map/while/body/eval_jaxpr/tile | solution.py:26
  657.7 22.9 %slice.31 = bf16[128,131328]{0,1:T(8,128)(2,1)} slice(bf16[128,131584]{0,1:T(8,128)(2,1)} %bitcast.32), slice={[0:128], [0:131328]} | slice | bytes 67239936 | tf_op jit(solution)/shard_map/while/body/eval_jaxpr/slice | solution.py:28
  680.5 37.7 %reshape.25 = bf16[128,256,513]{0,2,1:T(8,128)(2,1)} reshape(bf16[128,131328]{0,1:T(8,128)(2,1)} %slice.31) | data formatting | bytes 67239936 | tf_op jit(solution)/shard_map/while/body/eval_jaxpr/reshape | solution.py:28
  718.2 8.9 %fusion.22 = f32[4,16,256]{2,1,0:T(8,128)} fusion(f32[4,16,256]{2,1,0:T(8,128)} %get-tuple-element.83, s32[]{:T(128)} %get-tuple-element.82, bf16[128,16,256]{0,1,2:T(8,128)(2,1)S(1)} %get-tuple-element.91, bf16[128,256,513]{0,2,1:T(8,128)(2,1)} %reshape.25), kind=kOutput, calls=%fused_computation.3.clone.1 | convolution fusion | flops 268435456 | bytes 17842688 | tf_op jit(solution)/shard_map/while/body/eval_jaxpr/spk,skt->pt/dot_general | solution.py:51
  727.1 7.6 %psum.7 = f32[]{:T(128)} all-reduce(f32[]{:T(128)} %get-tuple-element.49), channel_id=1, replica_groups=mesh['sens'=4,'par'=64] {'sens'}, use_global_device_ids=true, to_apply=%region_5.6 | all-reduce | flops 1 | bytes 8 | tf_op jit(solution)/shard_map/psum | solution.py:46
  735.3 11.8 %reduce-scatter.2.cloned.1.call-done = f32[1,16,256]{2,1,0:T(8,128)} async-done(((f32[4,16,256]{2,1,0:T(8,128)}), f32[1,16,256]{2,1,0:T(8,128)}) %reduce-scatter.2.cloned.1.call-update) | async-done | bytes 16400 | tf_op jit(solution)/shard_map/reduce_scatter | solution.py:54
  (22 shorter events, 0.4 us)
Async XLA Ops:
  7.2 374.6 %all-gather.3.cloned.1.call-start = ((), (), s32[]{:S(2)}) async-start(), calls=%async_computation.2 | async-start | bytes 34078720 | tf_op jit(solution)/shard_map/all_gather | solution.py:8
  52.3 36.2 %copy-start = (bf16[128,16,256]{2,1,0:T(8,128)(2,1)S(1)}, bf16[128,16,256]{2,1,0:T(8,128)(2,1)}, u32[]{:S(2)}) copy-start(bf16[128,16,256]{2,1,0:T(8,128)(2,1)} %param.7) | copy-start | bytes 3145732
  95.3 651.9 %reduce-scatter.2.cloned.1.call-start = ((), (), s32[]{:S(2)}) async-start(), calls=%async_computation.1 | async-start | bytes 81920 | tf_op jit(solution)/shard_map/reduce_scatter | solution.py:54
  381.8 11.9 %copy-start.1 = (f32[4,128,256]{2,1,0:T(8,128)S(1)}, f32[4,128,256]{2,1,0:T(8,128)}, u32[]{:S(2)}) copy-start(f32[4,128,256]{2,1,0:T(8,128)} %param.8) | copy-start | bytes 1572868
  381.8 11.9 %copy-start.2 = (f32[128]{0:T(128)S(1)}, f32[128]{0:T(128)}, u32[]{:S(2)}) copy-start(f32[128]{0:T(128)} %param.9) | copy-start | bytes 1540
Sparse Core Ops, SparseCore 0:
  95.4 286.3 all-gather.2
  727.2 19.9 reduce-scatter.1
